TPU v7x, 32 devices: a whole 2x2x4 slice. The times are simulated.
32 devices in a mesh: chan: 4 (over z), frame: 8 (over y, x, core).
Axes of the slice: x: 2, y: 2, z: 4, core: 2. Of those that a mesh axis runs over, the one named last changes fastest.
Arguments:
- rf_data: bfloat16 [2, 8, 256, 1024], P(None, None, 'frame', 'chan'), may hold values from -6 to 6
- elem_pos: int32 [3, 1024], replicated, may hold values from -16 to 15, as said below
- vox_pos: int32 [3, 4096], P(None, 'chan'), may hold values from -32 to 62, as said below
- subbands: int32 [8], replicated, may hold values from 0 to 63, as said below
Outputs:
- filtered: bfloat16 [256, 2, 8, 4096], P('frame', None, None, 'chan')
Inputs may be any that keep to these rules, and one draw needn't show every extreme that they name: `elem_pos`: the element positions are the 32 x 32 grid with x and y from -16, each point once in a drawn order; z is 0, 1 or 2. `vox_pos`: distinct voxels of a box: x and y from -32 to 31, z from 48 to 62 in steps of 2. `subbands`: 8 distinct bin numbers.
All inputs are finite; a program needn't handle non-finite values.
Results may differ from a plain program's by a relative error of at most 0.0075.
Values may be sent and summed in bfloat16 or wider, within the bound.
A program may use at most 128 MiB of HBM per device.

v0:
```python
import functools
import math

import jax
import jax.numpy as jnp
from jax import lax
from jax.experimental import pallas as pl
from jax.experimental.pallas import tpu as pltpu
from jax.sharding import PartitionSpec as P

EPSILON = 1e-06
MESH = pl.DeviceIdType.MESH
F32 = jnp.float32
BF16 = jnp.bfloat16
SIN_POLY = (
    3.1415927410125732, -5.167710304260254, 2.550077438354492,
    -0.598291277885437, 0.07765766233205795,
)
COS_POLY = (
    0.9999999403953552, -4.934792995452881, 4.058411121368408,
    -1.331876516342163, 0.21968960762023926,
)
LANES = 128
ROUND = 12582912.0
GO_AT = 7


def horner(coefs, z):
    value = jnp.full_like(z, coefs[-1])
    for coef in coefs[-2::-1]:
        value = value * z + coef
    return value


def split(x):
    high = x.astype(BF16)
    return high, (x - high.astype(F32)).astype(BF16)


def dot(a, b):
    return jnp.dot(a, b, preferred_element_type=F32)


def dot_nt(a, b):
    return lax.dot_general(a, b, (((1,), (1,)), ((), ())), preferred_element_type=F32)


def kernel(
    nc, nf, nbins,
    rf_ref, elem_hbm, vox_hbm, sub_hbm, out_ref,
    rfbuf, elem_ref, vox_ref, sub_ref, in_sem, elem, vox, oper, acc, vols, part, slabs, total, sent,
    go_sem, own_sem, plane_send, plane_recv, right_send, right_recv, left_send, left_recv,
    rs_send, rs_recv, ag_send, ag_recv, out_own, out_send, out_recv,
):
    share = nf // nbins
    frames = rfbuf.shape[2]
    cl = rfbuf.shape[3]
    chans = nc * cl
    vd = vols.shape[1]
    fl = frames // nf
    group = nc * share
    rows = frames // group
    me_c = lax.axis_index("chan")
    me_f = lax.axis_index("frame")
    me_bin = me_f // share
    me_sub = me_f % share
    me_g = me_c * share + me_sub

    def member(k):
        m = lax.rem(me_g + k, group)
        return m, (m // share, me_bin * share + m % share)

    def planar(k):
        j = lax.rem(me_f + k, nf)
        return j, (me_c, j)

    barrier = pltpu.get_barrier_semaphore()
    for k in range(1, nf):
        pl.semaphore_signal(barrier, inc=1, device_id=planar(k)[1], device_id_type=MESH)
    for k in range(1, nc):
        for s in range(share):
            other = (lax.rem(me_c + k, nc), me_bin * share + s)
            pl.semaphore_signal(barrier, inc=1, device_id=other, device_id_type=MESH)

    def piece(j):
        return pl.ds(pl.multiple_of(j * fl, fl), fl)

    mine = piece(me_f)
    own = pltpu.make_async_copy(rf_ref.at[:, me_bin], rfbuf.at[me_c, :, mine], own_sem)
    own.start()
    loads = [
        pltpu.make_async_copy(source, place, in_sem.at[index])
        for index, (source, place) in enumerate(
            ((elem_hbm, elem_ref), (vox_hbm, vox_ref), (sub_hbm, sub_ref)))
    ]
    for load in loads:
        load.start()
    own.wait()
    pl.semaphore_wait(barrier, nf - 1 + (nc - 1) * share)

    def plane_copy(k):
        j, device = planar(k)
        return pltpu.make_async_remote_copy(
            src_ref=rf_ref.at[:, j // share], dst_ref=rfbuf.at[me_c, :, mine],
            send_sem=plane_send.at[j], recv_sem=plane_recv.at[me_f],
            device_id=device, device_id_type=MESH)

    def plane_arrival(j):
        return pltpu.make_async_remote_copy(
            src_ref=rf_ref.at[:, 0], dst_ref=rfbuf.at[me_c, :, piece(j)], send_sem=plane_send.at[j],
            recv_sem=plane_recv.at[j], device_id=(me_c, j), device_id_type=MESH)

    for k in range(1, nf):
        plane_copy(k).start()

    inverse = 1.0 / math.sqrt(chans)

    def block_of(k):
        return lax.rem(me_c + k + nc, nc)

    def make_operator(block, offset, count):
        @pl.loop(0, count)
        def _(step):
            place = pl.ds(pl.multiple_of(block * cl + (offset + step) * 16, 16), 16)
            ex, ey, ez = elem[0, place, :], elem[1, place, :], elem[2, place, :]
            for base in range(0, vd, LANES):
                lanes = slice(base, base + LANES)
                vz = vox[2:3, lanes]
                dx, dy, dz = vox[0:1, lanes] - ex, vox[1:2, lanes] - ey, vz - ez
                square = dx * dx + dy * dy + dz * dz
                inv = lax.rsqrt(square)
                inv = inv * (1.5 - (0.5 * square) * (inv * inv))
                turns = wavenum * (vz + square * inv)
                turns = turns - ((turns + ROUND) - ROUND)
                z = turns * turns
                sine = turns * horner(SIN_POLY, z)
                cosine = horner(COS_POLY, z)
                weight = dz * inv * inverse
                twice = (weight + weight) * sine
                oper[0, place, lanes] = (weight - twice * sine).astype(BF16)
                oper[1, place, lanes] = (twice * cosine).astype(BF16)

    def multiply(block, first=False, last=False):
        place = pl.ds(pl.multiple_of(block * cl, cl), cl)
        real, imag = rfbuf[block, 0], rfbuf[block, 1]
        upper = jnp.concatenate([real, imag], axis=1)
        lower = jnp.concatenate([imag, -real], axis=1)
        width = min(256, vd)

        @pl.loop(0, vd // width)
        def _(step):
            lanes = pl.ds(pl.multiple_of(step * width, width), width)
            both = jnp.concatenate([oper[0, place, lanes], oper[1, place, lanes]], axis=0)
            for half, left in enumerate((upper, lower)):
                where = slice(half * frames, (half + 1) * frames)
                value = dot(left, both)
                if not first:
                    value = value + acc[where, lanes]
                if last:
                    vols[where, lanes] = value.astype(BF16)
                else:
                    acc[where, lanes] = value

    right = (lax.rem(me_c + 1, nc), me_f)
    left = (lax.rem(me_c + nc - 1, nc), me_f)
    steps = nc // 2

    def ring_copy(step, j, rightward, arriving):
        sign = -1 if rightward else 1
        block = block_of(sign * (step if arriving else step - 1))
        ref = rfbuf.at[block, :, piece(j)]
        if step == steps:
            ref = rfbuf.at[block, 0 if rightward else 1, piece(j)]
        sends, recvs = (right_send, right_recv) if rightward else (left_send, left_recv)
        index = (step - 1) * nf + j
        return pltpu.make_async_remote_copy(
            src_ref=ref, dst_ref=ref, send_sem=sends.at[index], recv_sem=recvs.at[index],
            device_id=right if rightward else left, device_id_type=MESH)

    stagger = share == 1 and nf % 2 == 0
    second = lax.rem(me_f, 2) == 1

    def unless_second(run):
        if stagger:
            pl.when(jnp.logical_not(second))(run)
        else:
            run()

    def send_own():
        for rightward in (True, False):
            ring_copy(1, me_f, rightward, False).start()

    def let_go():
        pl.semaphore_signal(go_sem, inc=1, device_id=(me_c, me_f + 1), device_id_type=MESH)

    unless_second(send_own)
    for load in loads:
        load.wait()
    vstart = pl.multiple_of(me_sub * vd, LANES)
    vox[...] = vox_ref[:, pl.ds(vstart, vd)].astype(F32)
    for axis in range(3):
        for base in range(0, chans, LANES):
            row = elem_ref[axis:axis + 1, base:base + LANES].astype(F32)
            elem[axis, base:base + LANES, :] = jnp.broadcast_to(row, (LANES, LANES)).T
    wavenum = (32.0 + sub_ref[me_bin].astype(F32)) / 64.0

    tall = cl // 16
    portion = 2 * tall // nf

    def portion_of_operator(phase, k):
        at = k * portion
        later = at >= tall
        block = jnp.where(later, block_of(-phase - 1), block_of(phase))
        make_operator(block, jnp.where(later, at - tall, at), portion)

    if stagger:
        @pl.when(second)
        def _():
            make_operator(0, 0, nc * tall)
            pl.semaphore_wait(go_sem, 1)
            send_own()

    unless_second(lambda: portion_of_operator(0, 0))

    @pl.loop(1, nf)
    def _(k):
        j = lax.rem(me_f - k + nf, nf)
        plane_arrival(j).wait_recv()
        for rightward in (True, False):
            ring_copy(1, j, rightward, False).start()
        unless_second(lambda: portion_of_operator(0, k))

    if stagger and steps == 1:
        unless_second(let_go)

    for step in range(1, steps):
        if step == 2:
            multiply(me_c, first=True)
        if step > 1:
            multiply(block_of(1 - step))
            multiply(block_of(step - 1))

        @pl.loop(0, nf)
        def _(k):
            j = lax.rem(me_f - k + nf, nf)
            for rightward in (True, False):
                ring_copy(step, j, rightward, True).wait_recv()
                ring_copy(step + 1, j, rightward, False).start()
            if stagger and step == steps - 1:
                @pl.when(jnp.logical_and(jnp.logical_not(second), k == GO_AT * nf // 8))
                def _():
                    let_go()

            unless_second(lambda: portion_of_operator(step, k))

    if steps <= 2:
        multiply(me_c, first=True)
    if steps > 1:
        multiply(block_of(1 - steps))
        multiply(block_of(steps - 1))

    @pl.loop(0, nf)
    def _(k):
        j = lax.rem(me_f - k + nf, nf)
        for rightward in (True, False):
            ring_copy(steps, j, rightward, True).wait_recv()

    multiply(block_of(steps), last=True)

    real, imag = vols[:frames, :], vols[frames:, :]
    both = jnp.concatenate([real, imag], axis=1)
    gram_re = dot_nt(both, both)
    gram_im = dot_nt(jnp.concatenate([real, -imag], axis=1), jnp.concatenate([imag, real], axis=1))
    across = lax.broadcasted_iota(jnp.int32, (frames, frames), 1)
    down = lax.broadcasted_iota(jnp.int32, (frames, frames), 0)
    part[...] = jnp.where(down <= across, gram_re, gram_im).astype(BF16)

    def slab_of(m):
        return pl.ds(pl.multiple_of(m * rows, rows), rows)

    def scatter(k):
        m, device = member(k)
        return pltpu.make_async_remote_copy(
            src_ref=part.at[slab_of(m)], dst_ref=slabs.at[me_g],
            send_sem=rs_send.at[m], recv_sem=rs_recv.at[me_g],
            device_id=device, device_id_type=MESH)

    def scatter_arrival(k):
        m, device = member(k)
        return pltpu.make_async_remote_copy(
            src_ref=part.at[slab_of(m)], dst_ref=slabs.at[m],
            send_sem=rs_send.at[m], recv_sem=rs_recv.at[m],
            device_id=device, device_id_type=MESH)

    def gather(k, arriving=False):
        m, device = member(k)
        source = m if arriving else me_g
        return pltpu.make_async_remote_copy(
            src_ref=total.at[slab_of(source)], dst_ref=total.at[slab_of(source)],
            send_sem=ag_send.at[m], recv_sem=ag_recv.at[source],
            device_id=device, device_id_type=MESH)

    for k in range(1, group):
        scatter(k).start()
    summed = part[slab_of(me_g), :].astype(F32)
    for k in range(1, group):
        scatter_arrival(k).wait_recv()
        summed = summed + slabs[member(k)[0]].astype(F32)
    total[slab_of(me_g), :] = summed.astype(BF16)
    for k in range(1, group):
        gather(k).start()
    for k in range(1, group):
        gather(k, True).wait_recv()

    packed = total[...].astype(F32)
    turned = packed.T
    mat_re = jnp.where(down <= across, packed, turned)
    mat_im = jnp.where(down > across, packed, jnp.where(down < across, -turned, 0.0))
    squares = jnp.sum(jnp.sum(mat_re * mat_re + mat_im * mat_im, axis=1, keepdims=True), axis=0, keepdims=True)
    factor = 4.0 / jnp.sqrt(squares + EPSILON)
    mat_re = mat_re * factor
    mat_im = mat_im * factor
    rhs = jnp.concatenate(
        [jnp.concatenate([mat_re, mat_im], axis=1), jnp.concatenate([-mat_im, mat_re], axis=1)], axis=0)
    rhs_high, rhs_low = split(rhs)

    def product(pair):
        high, low = split(pair)
        return dot(high, rhs_high) + (dot(high, rhs_low) + dot(low, rhs_high))

    first = jnp.concatenate([mat_re, mat_im], axis=1)
    second = product(first)
    third = product(second)
    poly = 0.3 * second - 0.03 * third - first
    acc[:frames, :frames] = jnp.where(down == across, 1.0, 0.0) + poly[:, :frames]
    acc[frames:, :frames] = poly[:, frames:]

    def out_copy(j):
        return pltpu.make_async_remote_copy(
            src_ref=sent.at[:, pl.ds(pl.multiple_of(j * fl, fl), fl)], dst_ref=out_ref.at[me_f],
            send_sem=out_send.at[j], recv_sem=out_recv.at[me_f],
            device_id=(me_c, j), device_id_type=MESH)

    chunks = 4
    per = nf // chunks
    height = per * fl
    my_chunk = me_f // per
    for step in range(1, chunks + 1):
        chunk = lax.rem(my_chunk + step, chunks)
        place = pl.ds(pl.multiple_of(chunk * height, height), height)
        below = pl.ds(pl.multiple_of(frames + chunk * height, height), height)
        h_re = acc[place, :frames].astype(BF16)
        h_im = acc[below, :frames].astype(BF16)
        lhs = jnp.concatenate(
            [jnp.concatenate([h_re, h_im], axis=1), jnp.concatenate([-h_im, h_re], axis=1)], axis=0)
        value = dot(lhs, vols[...]).astype(BF16)
        sent[0, place, :] = value[:height]
        sent[1, place, :] = value[height:]
        for q in range(per):
            j = chunk * per + q
            if step < chunks:
                out_copy(j).start()
            else:
                @pl.when(j != me_f)
                def _():
                    out_copy(j).start()
    own_out = pltpu.make_async_copy(sent.at[:, mine], out_ref.at[me_f], out_own)
    own_out.start()
    for k in range(1, nf):
        plane_copy(k).wait_send()
    for step in range(1, steps + 1):
        @pl.loop(0, nf)
        def _(j):
            for rightward in (True, False):
                ring_copy(step, j, rightward, False).wait_send()

    for k in range(1, group):
        scatter(k).wait_send()
        gather(k).wait_send()
    own_out.wait()
    for k in range(1, nf):
        j, device = planar(k)
        pltpu.make_async_remote_copy(
            src_ref=sent.at[:, mine], dst_ref=out_ref.at[j], send_sem=out_send.at[j],
            recv_sem=out_recv.at[j], device_id=device, device_id_type=MESH).wait()


def shards(nc, nf, rf_data, elem_pos, vox_pos, subbands):
    nbins, fl, cl = rf_data.shape[1:]
    frames = fl * nf
    chans = cl * nc
    share = nf // nbins
    vl = vox_pos.shape[1]
    vd = vl // share
    group = nc * share
    steps = nc // 2
    dma = pltpu.SemaphoreType.DMA
    received = pl.pallas_call(
        functools.partial(kernel, nc, nf, nbins),
        out_shape=jax.ShapeDtypeStruct((nf, 2, fl, vd), BF16),
        in_specs=[pl.BlockSpec(memory_space=pl.ANY)] * 4,
        out_specs=pl.BlockSpec(memory_space=pl.ANY),
        scratch_shapes=[
            pltpu.VMEM((nc, 2, frames, cl), BF16),
            pltpu.VMEM(elem_pos.shape, elem_pos.dtype),
            pltpu.VMEM(vox_pos.shape, vox_pos.dtype),
            pltpu.SMEM(subbands.shape, subbands.dtype),
            dma((3,)),
            pltpu.VMEM((3, chans, LANES), F32),
            pltpu.VMEM((3, vd), F32),
            pltpu.VMEM((2, chans, vd), BF16),
            pltpu.VMEM((2 * frames, vd), F32),
            pltpu.VMEM((2 * frames, vd), BF16),
            pltpu.VMEM((frames, frames), BF16),
            pltpu.VMEM((group, frames // group, frames), BF16),
            pltpu.VMEM((frames, frames), BF16),
            pltpu.VMEM((2, frames, vd), BF16),
            pltpu.SemaphoreType.REGULAR, dma, dma((nf,)), dma((nf,)),
            dma((steps * nf,)), dma((steps * nf,)), dma((steps * nf,)), dma((steps * nf,)),
            dma((group,)), dma((group,)), dma((group,)), dma((group,)),
            dma, dma((nf,)), dma((nf,)),
        ],
        compiler_params=pltpu.CompilerParams(
            collective_id=0, has_side_effects=True, vmem_limit_bytes=60 * 2**20),
    )(rf_data, elem_pos, vox_pos, subbands)
    received = received.reshape(nbins, share, 2, fl, vd)
    return jnp.transpose(received, (3, 2, 0, 1, 4)).reshape(fl, 2, nbins, vl)


def solution(mesh):
    return jax.shard_map(
        functools.partial(shards, mesh.shape["chan"], mesh.shape["frame"]),
        mesh=mesh,
        in_specs=(P(None, None, "frame", "chan"), P(), P(None, "chan"), P()),
        out_specs=P("frame", None, None, "chan"),
        check_vma=False,
    )
```

profile of v0, /device:TPU:1, one launch (start us, length us, event | category | flops | bytes accessed | tf_op | source)
XLA Modules:
  0.0 50.8 jit_solution(16618112349684365973)
XLA Ops:
  0.0 48.0 %shard_map.46 = bf16[8,2,32,1024]{3,2,1,0:T(8,128)(2,1)} custom-call(bf16[2,8,32,256]{3,2,1,0:T(8,128)(2,1)} %rf_ref.1, s32[3,1024]{1,0:T(4,128)} %elem_hbm.1, s32[3,1024]{1,0:T(4,128)} %vox_hbm.1, s32[8]{0:T(128)} %sub_hbm.1), custom_call_target="tpu_custom_call" | custom-call | tf_op jit(solution)/shard_map/pallas_call | solution.py:398
  48.0 2.8 %copy.5 = bf16[32,2,8,1024]{3,2,1,0:T(8,128)(2,1)} copy(bf16[32,2,8,1024]{3,0,1,2:T(8,128)(2,1)} %bitcast.5) | data formatting | bytes 2097152 | tf_op jit(solution)/shard_map/reshape | solution.py:427
where the time goes:
time: 51 us; the launch traced here: 50.8 us
  Pallas kernels  48 us (94%)
  local copies, waits for them, and re-layouts  2.77 us (5%)
    pallas_call x1, Pallas kernels, shards(): pl.pallas_call(functools.partial(kernel, nc, nf, nbins), out_shape=jax.Sh...  48 us
    reshape x1, local copies, waits for them, and re-layouts, shards(): return jnp.transpose(received, (3, 2, 0, 1, 4)).reshape(fl, 2, nbins, vl)  2.77 us

commit v1 on v0

v1 whole, which is shorter than its diff:
```python
import functools
import math

import jax
import jax.numpy as jnp
from jax import lax
from jax.experimental import pallas as pl
from jax.experimental.pallas import tpu as pltpu
from jax.sharding import PartitionSpec as P

EPSILON = 1e-06
MESH = pl.DeviceIdType.MESH
F32 = jnp.float32
BF16 = jnp.bfloat16
SIN_POLY = (3.1415820121765137, -5.167142868041992, 2.5418989658355713, -0.5546361804008484)
COS_POLY = (0.9999933242797852, -4.933938026428223, 4.04128360748291, -1.222127079963684)
LANES = 128
ROUND = 12582912.0
TALL = 16
REACH = 2
GO_AT = 7


def horner(coefs, z):
    value = coefs[-1] * z + coefs[-2]
    for coef in coefs[-3::-1]:
        value = value * z + coef
    return value


def dot(a, b):
    return jnp.dot(a, b, preferred_element_type=F32)


def dot_nt(a, b):
    return lax.dot_general(a, b, (((1,), (1,)), ((), ())), preferred_element_type=F32)


def kernel(
    nc, nf, nbins,
    rf_ref, elem_hbm, vox_hbm, sub_hbm, out_ref,
    rfbuf, elem_ref, vox_ref, sub_ref, in_sem, elem, vox, oper, acc, vols, part, slabs, total, hmat, sent,
    go_sem, own_sem, plane_send, plane_recv, line_send, relay_send, line_recv,
    rs_send, rs_recv, ag_send, ag_recv, out_own, out_send, out_recv,
):
    share = nf // nbins
    stagger = share == 1 and nf % 2 == 0
    frames = rfbuf.shape[2]
    cl = rfbuf.shape[3]
    chans = nc * cl
    vd = vols.shape[1]
    fl = frames // nf
    halves = nf // 2
    width = vd // halves
    rows = frames // 2
    owners = ((nc // 2 - 1, 0), (nc // 2, 0))
    me_c = lax.axis_index("chan")
    me_f = lax.axis_index("frame")
    me_bin = lax.div(me_f, share)
    me_sub = lax.rem(me_f, share)
    second = lax.rem(me_f, 2) == 1
    first_core = jnp.logical_not(second)
    def partner(k):
        j = 0
        bit = 1
        while bit < nf:
            a = lax.rem(lax.div(me_f, bit), 2)
            b = k // bit % 2 if isinstance(k, int) else lax.rem(lax.div(k, bit), 2)
            j = j + bit * (a + b - 2 * a * b)
            bit *= 2
        return j

    def if_first(run, *conditions):
        for condition in conditions + ((first_core,) if stagger else ()):
            run = functools.partial(pl.when(condition), run)
        run()

    def piece(j):
        return pl.ds(pl.multiple_of(j * fl, fl), fl)

    barrier = pltpu.get_barrier_semaphore()
    for k in range(1, nf):
        pl.semaphore_signal(barrier, inc=1, device_id=(me_c, partner(k)), device_id_type=MESH)
    for k in range(1, nc):
        for s in range(share):
            other = (lax.rem(me_c + k, nc), me_bin * share + s)
            pl.semaphore_signal(barrier, inc=1, device_id=other, device_id_type=MESH)

    mine = piece(me_f)
    loads = [
        pltpu.make_async_copy(source, place, in_sem.at[index])
        for index, (source, place) in enumerate(
            ((elem_hbm, elem_ref), (vox_hbm, vox_ref), (sub_hbm, sub_ref)))
    ]
    for load in loads:
        load.start()
    own = pltpu.make_async_copy(rf_ref.at[:, me_bin], rfbuf.at[me_c, :, mine], own_sem)
    own.start()
    pl.semaphore_wait(barrier, nf - 1 + (nc - 1) * share)

    def plane_copy(j):
        return pltpu.make_async_remote_copy(
            src_ref=rf_ref.at[:, lax.div(j, share)], dst_ref=rfbuf.at[me_c, :, mine],
            send_sem=plane_send.at[j], recv_sem=plane_recv.at[me_f],
            device_id=(me_c, j), device_id_type=MESH)

    def plane_arrival(j):
        return pltpu.make_async_remote_copy(
            src_ref=rf_ref.at[:, 0], dst_ref=rfbuf.at[me_c, :, piece(j)], send_sem=plane_send.at[j],
            recv_sem=plane_recv.at[j], device_id=(me_c, j), device_id_type=MESH)

    def line_copy(block, j, target, send_sem, mine_too=False):
        place = rfbuf.at[block, :, piece(j)]
        return pltpu.make_async_remote_copy(
            src_ref=rf_ref.at[:, me_bin] if mine_too else place, dst_ref=place,
            send_sem=send_sem, recv_sem=line_recv.at[block * nf + j],
            device_id=(target, me_f), device_id_type=MESH)

    def own_copy(j, offset, mine_too=False):
        slot = offset + REACH - (offset > 0)
        return line_copy(me_c, j, me_c + offset, line_send.at[slot * nf + j], mine_too)

    def relay_copy(block, j):
        target = jnp.where(block < me_c, me_c + 1, me_c - 1)
        return line_copy(block, j, target, relay_send.at[block * nf + j])

    def there(offset):
        return me_c + offset < nc if offset > 0 else me_c + offset >= 0

    def send_far(j, mine_too=False):
        for offset in range(REACH, 0, -1):
            for signed in (offset, -offset):
                farther = signed + (1 if signed > 0 else -1)
                condition = there(signed)
                if offset < REACH:
                    condition = jnp.logical_and(condition, jnp.logical_not(there(farther)))

                @pl.when(condition)
                def _():
                    own_copy(j, signed, mine_too).start()

    def send_near(j, mine_too=False):
        for offset in range(REACH - 1, 0, -1):
            for signed in (offset, -offset):
                @pl.when(there(signed + (1 if signed > 0 else -1)))
                def _():
                    own_copy(j, signed, mine_too).start()

    if_first(lambda: send_far(me_f, True))
    base_f = me_f - lax.rem(me_f, 2)
    for parity in (0, 1):
        for k in range(0, nf, 2):
            j = lax.rem(base_f + k, nf) + parity
            if k == 0:
                @pl.when(j != me_f)
                def _():
                    plane_copy(j).start()
            else:
                plane_copy(j).start()

    inverse = 2.0 / math.sqrt(chans)
    for load in loads:
        load.wait()
    vox[...] = vox_ref[:, pl.ds(pl.multiple_of(me_sub * vd, LANES), vd)].astype(F32)
    for axis in range(3):
        for base in range(0, chans, LANES):
            row = elem_ref[axis:axis + 1, base:base + LANES].astype(F32)
            elem[axis, base:base + LANES, :] = jnp.broadcast_to(row, (LANES, LANES)).T
    wavenum = (32.0 + sub_ref[me_bin].astype(F32)) / 64.0

    tall = cl // TALL
    steps = nc * tall

    def make_operator(low, high):
        @pl.loop(low, high)
        def _(step):
            block = lax.rem(me_c + lax.div(step, tall), nc)
            place = pl.ds(pl.multiple_of(block * cl + lax.rem(step, tall) * TALL, TALL), TALL)
            ex, ey, ez = elem[0, place, :], elem[1, place, :], elem[2, place, :]
            for base in range(0, vd, LANES):
                lanes = slice(base, base + LANES)
                vz = vox[2:3, lanes]
                dx, dy, dz = vox[0:1, lanes] - ex, vox[1:2, lanes] - ey, vz - ez
                square = dx * dx + dy * dy + dz * dz
                inv = lax.rsqrt(square)
                turns = wavenum * (vz + square * inv)
                turns = turns - ((turns + ROUND) - ROUND)
                z = turns * turns
                sine = turns * horner(SIN_POLY, z)
                cosine = horner(COS_POLY, z)
                twice = dz * inverse * inv
                oper[0, place, lanes] = (twice * (0.5 - sine * sine)).astype(BF16)
                oper[1, place, lanes] = (twice * sine * cosine).astype(BF16)

    def multiply_step(block, step, first=False, last=False):
        place = pl.ds(pl.multiple_of(block * cl, cl), cl)
        real, imag = rfbuf[block, 0], rfbuf[block, 1]
        left = jnp.concatenate(
            [jnp.concatenate([real, imag], axis=1), jnp.concatenate([imag, -real], axis=1)], axis=0)
        lanes = pl.ds(pl.multiple_of(step * width, width), width)
        value = dot(left, jnp.concatenate([oper[0, place, lanes], oper[1, place, lanes]], axis=0))
        if not first:
            value = value + acc[:, lanes]
        if last:
            vols[:, lanes] = value.astype(BF16)
        else:
            acc[:, lanes] = value

    def multiply(block, first=False, last=False):
        @pl.loop(0, halves)
        def _(step):
            multiply_step(block, step, first, last)

    def passed_on(block):
        right = jnp.logical_and(me_c - block >= REACH, me_c < nc - 1)
        return jnp.logical_or(right, jnp.logical_and(block - me_c >= REACH, me_c > 0))

    begin = steps // 8
    portion = (steps - begin) * 3 // 8 // (nf - 1)
    rest = begin + portion * (nf - 1)

    def let_go():
        pl.semaphore_signal(go_sem, inc=1, device_id=(me_c, me_f + 1), device_id_type=MESH)

    def run_second():
        make_operator(0, steps)

        @pl.loop(1, nf)
        def _(k):
            plane_arrival(partner(k)).wait_recv()

        own.wait()
        multiply(me_c, first=True)
        pl.semaphore_wait(go_sem, 1)

        @pl.loop(0, nf)
        def _(k):
            send_far(partner(k))

        @pl.loop(0, nf)
        def _(k):
            send_near(partner(k))

    def run_first():
        make_operator(0, begin)

        @pl.loop(1, nf)
        def _(k):
            j = partner(k)
            plane_arrival(j).wait_recv()
            send_far(j)
            make_operator(begin + (k - 1) * portion, begin + k * portion)

        send_near(me_f, True)

        @pl.loop(1, nf)
        def _(k):
            send_near(partner(k))

        own.wait()

    if stagger:
        pl.when(second)(run_second)
    if_first(run_first)

    @pl.loop(REACH, nc - 1)
    def _(hop):
        block = jnp.where(me_c >= hop, me_c - hop, me_c + hop)
        other = jnp.where(me_c >= hop, me_c + hop, nc)

        @pl.loop(0, nf)
        def _(k):
            j = partner(k)
            for which in (block, other):
                @pl.when(jnp.logical_and(which < nc, passed_on(which)))
                def _():
                    relay_copy(which, j).wait_recv()
                    relay_copy(which, j).start()

            def early():
                @pl.when(k < halves)
                def _():
                    make_operator(rest + lax.div((steps - rest) * k, halves), rest + lax.div((steps - rest) * (k + 1), halves))

                @pl.when(k >= halves)
                def _():
                    multiply_step(me_c, k - halves, first=True)

            if_first(early, hop == REACH)
            if stagger:
                if_first(let_go, hop == REACH, k == GO_AT * nf // 8)

    if nc <= REACH + 1:
        if_first(lambda: make_operator(rest, steps))
        if_first(lambda: multiply(me_c, first=True))
        if stagger:
            if_first(let_go)

    lower = 2 * me_c < nc
    depth = jnp.where(lower, me_c, nc - 1 - me_c)

    def block_in_turn(turn):
        place = jnp.where(turn <= depth, depth - turn, nc + depth - turn)
        place = jnp.where(depth == 0, turn, place)
        return jnp.where(lower, place, nc - 1 - place)

    def arrive(block):
        @pl.when(jnp.logical_not(passed_on(block)))
        def _():
            @pl.loop(0, nf)
            def _(k):
                j = partner(k)
                line_copy(block, j, block, relay_send.at[block * nf + j]).wait_recv()

    @pl.loop(1, nc - 1)
    def _(turn):
        block = block_in_turn(turn)
        arrive(block)
        multiply(block)

    arrive(block_in_turn(nc - 1))
    multiply(block_in_turn(nc - 1), last=True)

    real, imag = vols[:frames, :], vols[frames:, :]
    both = jnp.concatenate([real, imag], axis=1)
    gram_re = dot_nt(both, both)
    gram_im = dot_nt(jnp.concatenate([real, -imag], axis=1), jnp.concatenate([imag, real], axis=1))
    across = lax.broadcasted_iota(jnp.int32, (frames, frames), 1)
    down = lax.broadcasted_iota(jnp.int32, (frames, frames), 0)
    part[...] = jnp.where(down <= across, gram_re, gram_im).astype(BF16)

    members = [(c, t) for c in range(nc) for t in range(share)]

    def device(member):
        return member[0], me_bin * share + member[1]

    def is_me(member):
        return jnp.logical_and(me_c == member[0], me_sub == member[1])

    def half(index):
        return pl.ds(index * rows, rows)

    def scatter(index, source=None):
        origin = me_c * share + me_sub if source is None else members.index(source)
        return pltpu.make_async_remote_copy(
            src_ref=part.at[half(index)], dst_ref=slabs.at[origin],
            send_sem=rs_send.at[index], recv_sem=rs_recv.at[origin],
            device_id=device(owners[index]), device_id_type=MESH)

    def gather(index, member):
        place = total.at[half(index)]
        return pltpu.make_async_remote_copy(
            src_ref=place, dst_ref=place, send_sem=ag_send.at[members.index(member)], recv_sem=ag_recv.at[index],
            device_id=device(member), device_id_type=MESH)

    upper_half = 2 * me_c >= nc
    for turn in range(2):
        for index in range(2):
            across_line = upper_half if index == 0 else jnp.logical_not(upper_half)
            chosen = across_line if turn == 0 else jnp.logical_not(across_line)

            @pl.when(jnp.logical_and(chosen, jnp.logical_not(is_me(owners[index]))))
            def _():
                scatter(index).start()
    for index in range(2):
        @pl.when(is_me(owners[index]))
        def _():
            others = sorted(
                (m for m in members if m != owners[index]), key=lambda m: abs(m[0] - owners[index][0]))
            summed = part[half(index), :].astype(F32)
            for member in others:
                scatter(index, member).wait_recv()
                summed = summed + slabs[members.index(member)].astype(F32)
            total[half(index), :] = summed.astype(BF16)
            for member in others[::-1]:
                gather(index, member).start()
    for index in range(2):
        @pl.when(jnp.logical_not(is_me(owners[index])))
        def _():
            gather(index, owners[index]).wait_recv()

    packed = total[...].astype(F32)
    turned = packed.T
    same = down == across
    g_re = jnp.where(down <= across, packed, turned)
    g_im = jnp.where(down > across, packed, jnp.where(same, 0.0, -turned))
    squares = packed * packed
    squares = jnp.where(same, squares, squares + squares)
    squares = jnp.sum(jnp.sum(squares, axis=0, keepdims=True), axis=1, keepdims=True)
    factor = 4.0 / jnp.sqrt(squares + EPSILON)
    first = jnp.concatenate([g_re, g_im], axis=1).astype(BF16)
    below = jnp.concatenate([-g_im, g_re], axis=1).astype(BF16)
    rhs = jnp.concatenate([first, below], axis=0)
    second_power = dot(first, rhs)
    high = second_power.astype(BF16)
    low = (second_power - high.astype(F32)).astype(BF16)
    third_power = dot(high, rhs) + dot(low, rhs)
    poly = factor * (factor * (0.3 * second_power - (0.03 * factor) * third_power) - first.astype(F32))
    h_re = (jnp.where(same, 1.0, 0.0) + poly[:, :frames]).astype(BF16)
    h_im = poly[:, frames:].astype(BF16)
    hmat[:frames, :frames] = h_re
    hmat[:frames, frames:] = h_im
    hmat[frames:, :frames] = -h_im
    hmat[frames:, frames:] = h_re

    def out_copy(j, chunk):
        lanes = pl.ds(chunk * span, span)
        return pltpu.make_async_remote_copy(
            src_ref=sent.at[:, piece(j), lanes], dst_ref=out_ref.at[me_f, :, :, lanes],
            send_sem=out_send.at[chunk * nf + j], recv_sem=out_recv.at[chunk * nf + me_f],
            device_id=(me_c, j), device_id_type=MESH)

    chunks = out_own.shape[0]
    span = vd // chunks
    lhs = hmat[...]
    for chunk in range(chunks):
        lanes = pl.ds(chunk * span, span)
        value = dot(lhs, vols[:, lanes]).astype(BF16)
        sent[0, :, lanes] = value[:frames]
        sent[1, :, lanes] = value[frames:]
        for k in range(nf - 1, 0, -1):
            out_copy(partner(k), chunk).start()
        pltpu.make_async_copy(sent.at[:, mine, lanes], out_ref.at[me_f, :, :, lanes], out_own.at[chunk]).start()

    @pl.loop(1, nf)
    def _(k):
        plane_copy(partner(k)).wait_send()

    @pl.loop(0, nf)
    def _(j):
        for offset in range(1, REACH + 1):
            for signed in (offset, -offset):
                @pl.when(there(signed))
                def _():
                    own_copy(j, signed).wait_send()

        @pl.loop(0, nc)
        def _(block):
            @pl.when(passed_on(block))
            def _():
                relay_copy(block, j).wait_send()

    for index in range(2):
        @pl.when(jnp.logical_not(is_me(owners[index])))
        def _():
            scatter(index).wait_send()

        @pl.when(is_me(owners[index]))
        def _():
            for member in members:
                if member != owners[index]:
                    gather(index, member).wait_send()
    for chunk in range(chunks):
        lanes = pl.ds(chunk * span, span)
        pltpu.make_async_copy(sent.at[:, mine, lanes], out_ref.at[me_f, :, :, lanes], out_own.at[chunk]).wait()

        @pl.loop(1, nf)
        def _(k):
            j = partner(k)
            out_copy(j, chunk).wait_send()
            pltpu.make_async_remote_copy(
                src_ref=sent.at[:, mine, lanes], dst_ref=out_ref.at[j, :, :, lanes],
                send_sem=out_send.at[chunk * nf + j], recv_sem=out_recv.at[chunk * nf + j],
                device_id=(me_c, j), device_id_type=MESH).wait_recv()


def shards(nc, nf, rf_data, elem_pos, vox_pos, subbands):
    nbins, fl, cl = rf_data.shape[1:]
    frames = fl * nf
    chans = cl * nc
    share = nf // nbins
    vl = vox_pos.shape[1]
    vd = vl // share
    group = nc * share
    chunks = 4
    dma = pltpu.SemaphoreType.DMA
    inputs = [pltpu.with_memory_space_constraint(x, pltpu.HBM) for x in (rf_data, elem_pos, vox_pos, subbands)]
    received = pl.pallas_call(
        functools.partial(kernel, nc, nf, nbins),
        out_shape=pltpu.VMEM((nf, 2, fl, vd), BF16),
        in_specs=[pl.BlockSpec(memory_space=pl.ANY)] * 4,
        out_specs=pl.BlockSpec(memory_space=pl.ANY),
        scratch_shapes=[
            pltpu.VMEM((nc, 2, frames, cl), BF16),
            pltpu.VMEM(elem_pos.shape, elem_pos.dtype),
            pltpu.VMEM(vox_pos.shape, vox_pos.dtype),
            pltpu.SMEM(subbands.shape, subbands.dtype),
            dma((3,)),
            pltpu.VMEM((3, chans, LANES), F32),
            pltpu.VMEM((3, vd), F32),
            pltpu.VMEM((2, chans, vd), BF16),
            pltpu.VMEM((2 * frames, vd), F32),
            pltpu.VMEM((2 * frames, vd), BF16),
            pltpu.VMEM((frames, frames), BF16),
            pltpu.VMEM((group, frames // 2, frames), BF16),
            pltpu.VMEM((frames, frames), BF16),
            pltpu.VMEM((2 * frames, 2 * frames), BF16),
            pltpu.VMEM((2, frames, vd), BF16),
            pltpu.SemaphoreType.REGULAR, dma, dma((nf,)), dma((nf,)),
            dma((2 * REACH * nf,)), dma((nc * nf,)), dma((nc * nf,)),
            dma((2,)), dma((group,)), dma((group,)), dma((2,)),
            dma((chunks,)), dma((chunks * nf,)), dma((chunks * nf,)),
        ],
        compiler_params=pltpu.CompilerParams(
            collective_id=0, has_side_effects=True, vmem_limit_bytes=40 * 2**20),
    )(*inputs)
    received = received.reshape(nbins, share, 2, fl, vd)
    return jnp.transpose(received, (3, 2, 0, 1, 4)).reshape(fl, 2, nbins, vl)


def solution(mesh):
    return jax.shard_map(
        functools.partial(shards, mesh.shape["chan"], mesh.shape["frame"]),
        mesh=mesh,
        in_specs=(P(None, None, "frame", "chan"), P(), P(None, "chan"), P()),
        out_specs=P("frame", None, None, "chan"),
        check_vma=False,
    )
```

time: 51 us -> 48.3 us (0.947)
  Pallas kernels: 48 us -> 46.2 us
  local copies, waits for them, and re-layouts: 2.77 us -> 1.55 us
    pallas_call x1, Pallas kernels: 48 us -> 46.2 us  [shards(): pl.pallas_call(functools.partial(kernel, nc, nf, nbins), out_shape=pltpu....]
    reshape x1, local copies, waits for them, and re-layouts: 2.77 us -> 1.55 us  [shards(): return jnp.transpose(received, (3, 2, 0, 1, 4)).reshape(fl, 2, nbins, vl)]
where the time goes in v1:
time: 48.3 us; the launch traced here: 47.8 us
  Pallas kernels  46.2 us (96%)
  local copies, waits for them, and re-layouts  1.55 us (3%)
    pallas_call x1, Pallas kernels, shards(): pl.pallas_call(functools.partial(kernel, nc, nf, nbins), out_shape=pltpu....  46.2 us
    reshape x1, local copies, waits for them, and re-layouts, shards(): return jnp.transpose(received, (3, 2, 0, 1, 4)).reshape(fl, 2, nbins, vl)  1.55 us

profile of v1, /device:TPU:1, one launch (start us, length us, event | category | flops | bytes accessed | tf_op | source)
XLA Modules:
  0.0 47.8 jit_solution(6506026388626216644)
XLA Ops:
  0.0 46.2 %shard_map.46 = bf16[8,2,32,1024]{3,2,1,0:T(8,128)(2,1)S(1)} custom-call(bf16[2,8,32,256]{3,2,1,0:T(8,128)(2,1)} %rf_ref.1, s32[3,1024]{1,0:T(4,128)} %elem_hbm.1, s32[3,1024]{1,0:T(4,128)} %vox_hbm.1, s32[8]{0:T(128)} %sub_hbm.1), custom_call_target="tpu_custom_call" | custom-call | tf_op jit(solution)/shard_map/pallas_call | solution.py:478
  46.2 1.5 %copy.5 = bf16[32,2,8,1024]{3,2,1,0:T(8,128)(2,1)} copy(bf16[32,2,8,1024]{3,0,1,2:T(8,128)(2,1)S(1)} %bitcast.5) | data formatting | bytes 2097152 | tf_op jit(solution)/shard_map/reshape | solution.py:508

commit v2 on v1

--- a/solution.py
+++ b/solution.py
@@ -13,12 +13,13 @@
 F32 = jnp.float32
 BF16 = jnp.bfloat16
 SIN_POLY = (3.1415820121765137, -5.167142868041992, 2.5418989658355713, -0.5546361804008484)
-COS_POLY = (0.9999933242797852, -4.933938026428223, 4.04128360748291, -1.222127079963684)
+BELOW_ONE = 1.0 - 2e-6
 LANES = 128
 ROUND = 12582912.0
-TALL = 16
+TALL = 32
 REACH = 2
 GO_AT = 7
+SECOND_REACH = 1
 
 
 def horner(coefs, z):
@@ -39,7 +40,7 @@
 def kernel(
     nc, nf, nbins,
     rf_ref, elem_hbm, vox_hbm, sub_hbm, out_ref,
-    rfbuf, elem_ref, vox_ref, sub_ref, in_sem, elem, vox, oper, acc, vols, part, slabs, total, hmat, sent,
+    rfbuf, elem_ref, vox_ref, sub_ref, in_sem, elem, heights, vox, squares, oper, acc, vols, part, slabs, total, hmat, sent,
     go_sem, own_sem, plane_send, plane_recv, line_send, relay_send, line_recv,
     rs_send, rs_recv, ag_send, ag_recv, out_own, out_send, out_recv,
 ):
@@ -50,8 +51,6 @@
     chans = nc * cl
     vd = vols.shape[1]
     fl = frames // nf
-    halves = nf // 2
-    width = vd // halves
     rows = frames // 2
     owners = ((nc // 2 - 1, 0), (nc // 2, 0))
     me_c = lax.axis_index("chan")
@@ -70,6 +69,8 @@
             bit *= 2
         return j
 
+    reach = jnp.where(second, SECOND_REACH, REACH) if stagger else REACH
+
     def if_first(run, *conditions):
         for condition in conditions + ((first_core,) if stagger else ()):
             run = functools.partial(pl.when(condition), run)
@@ -158,15 +159,35 @@
             else:
                 plane_copy(j).start()
 
-    inverse = 2.0 / math.sqrt(chans)
+    scale = 2.0 / math.sqrt(chans)
+    sin_poly = [coef * math.sqrt(scale) * BELOW_ONE for coef in SIN_POLY]
     for load in loads:
         load.wait()
-    vox[...] = vox_ref[:, pl.ds(pl.multiple_of(me_sub * vd, LANES), vd)].astype(F32)
-    for axis in range(3):
-        for base in range(0, chans, LANES):
-            row = elem_ref[axis:axis + 1, base:base + LANES].astype(F32)
-            elem[axis, base:base + LANES, :] = jnp.broadcast_to(row, (LANES, LANES)).T
     wavenum = (32.0 + sub_ref[me_bin].astype(F32)) / 64.0
+    voxels = vox_ref[:, pl.ds(pl.multiple_of(me_sub * vd, LANES), vd)].astype(F32)
+    vx, vy, vz = voxels[0:1], voxels[1:2], voxels[2:3]
+    vox[...] = vz * wavenum
+    kind = lax.broadcasted_iota(jnp.int32, (8, vd), 0)
+    terms = jnp.where(kind == 0, vx, jnp.where(kind == 1, vy, vz)) * -2.0
+    terms = jnp.where(kind < 3, terms, jnp.where(kind == 3, vx * vx + vy * vy + vz * vz, 1.0)) * (wavenum * wavenum)
+    terms = jnp.where(kind < 6, terms, 0.0)
+    parts = []
+    for _ in range(3):
+        parts.append(terms.astype(BF16).astype(F32))
+        terms = terms - parts[-1]
+    right = jnp.concatenate(parts + [jnp.zeros((LANES - 24, vd), F32)], axis=0).astype(BF16)
+    kind = lax.broadcasted_iota(jnp.int32, (8, LANES), 0)
+    for base in range(0, chans, LANES):
+        points = elem_ref[:, base:base + LANES]
+        ex, ey, ez = points[0:1], points[1:2], points[2:3]
+        norm = ex * ex + ey * ey + ez * ez
+        low = jnp.bitwise_and(norm, 15)
+        facts = jnp.where(kind == 0, ex, jnp.where(kind == 1, ey, jnp.where(kind == 2, ez, 1)))
+        facts = jnp.where(kind < 4, facts, jnp.where(kind == 4, norm - low, jnp.where(kind == 5, low, 0))).astype(F32)
+        facts = jnp.concatenate([facts, facts, facts, jnp.zeros((LANES - 24, LANES), F32)], axis=0)
+        elem[base:base + LANES, :] = facts.T.astype(BF16)
+        heights[base:base + LANES, :] = jnp.broadcast_to(ez.astype(F32) * wavenum, (LANES, LANES)).T
+    squares[...] = dot(elem[...], right)
 
     tall = cl // TALL
     steps = nc * tall
@@ -176,48 +197,50 @@
         def _(step):
             block = lax.rem(me_c + lax.div(step, tall), nc)
             place = pl.ds(pl.multiple_of(block * cl + lax.rem(step, tall) * TALL, TALL), TALL)
-            ex, ey, ez = elem[0, place, :], elem[1, place, :], elem[2, place, :]
+            ez = heights[place, :]
             for base in range(0, vd, LANES):
                 lanes = slice(base, base + LANES)
-                vz = vox[2:3, lanes]
-                dx, dy, dz = vox[0:1, lanes] - ex, vox[1:2, lanes] - ey, vz - ez
-                square = dx * dx + dy * dy + dz * dz
+                vz, square = vox[:, lanes], squares[place, lanes]
                 inv = lax.rsqrt(square)
-                turns = wavenum * (vz + square * inv)
+                turns = vz + square * inv
                 turns = turns - ((turns + ROUND) - ROUND)
-                z = turns * turns
-                sine = turns * horner(SIN_POLY, z)
-                cosine = horner(COS_POLY, z)
-                twice = dz * inverse * inv
-                oper[0, place, lanes] = (twice * (0.5 - sine * sine)).astype(BF16)
+                sine = turns * horner(sin_poly, turns * turns)
+                rest = scale - sine * sine
+                cosine = rest * lax.rsqrt(rest)
+                twice = (vz - ez) * inv
+                oper[0, place, lanes] = (twice * (rest - 0.5 * scale)).astype(BF16)
                 oper[1, place, lanes] = (twice * sine * cosine).astype(BF16)
 
-    def multiply_step(block, step, first=False, last=False):
+    def multiply(block, first=False, last=False, part_of=None):
         place = pl.ds(pl.multiple_of(block * cl, cl), cl)
-        real, imag = rfbuf[block, 0], rfbuf[block, 1]
+        right = jnp.concatenate([oper[0, place, :], oper[1, place, :]], axis=0)
+        if part_of is None:
+            real, imag = rfbuf[block, 0], rfbuf[block, 1]
+            wheres = (slice(0, 2 * frames),)
+        else:
+            some = pl.ds(pl.multiple_of(part_of * rows, rows), rows)
+            real, imag = rfbuf[block, 0, some, :], rfbuf[block, 1, some, :]
+            wheres = (some, pl.ds(pl.multiple_of(frames + part_of * rows, rows), rows))
         left = jnp.concatenate(
             [jnp.concatenate([real, imag], axis=1), jnp.concatenate([imag, -real], axis=1)], axis=0)
-        lanes = pl.ds(pl.multiple_of(step * width, width), width)
-        value = dot(left, jnp.concatenate([oper[0, place, lanes], oper[1, place, lanes]], axis=0))
-        if not first:
-            value = value + acc[:, lanes]
-        if last:
-            vols[:, lanes] = value.astype(BF16)
-        else:
-            acc[:, lanes] = value
-
-    def multiply(block, first=False, last=False):
-        @pl.loop(0, halves)
-        def _(step):
-            multiply_step(block, step, first, last)
+        value = dot(left, right)
+        for index, where in enumerate(wheres):
+            some = value if part_of is None else value[index * rows:(index + 1) * rows]
+            if not first:
+                some = some + acc[where, :]
+            if last:
+                vols[where, :] = some.astype(BF16)
+            else:
+                acc[where, :] = some
 
     def passed_on(block):
-        right = jnp.logical_and(me_c - block >= REACH, me_c < nc - 1)
-        return jnp.logical_or(right, jnp.logical_and(block - me_c >= REACH, me_c > 0))
+        right = jnp.logical_and(me_c - block >= reach, me_c < nc - 1)
+        return jnp.logical_or(right, jnp.logical_and(block - me_c >= reach, me_c > 0))
 
     begin = steps // 8
-    portion = (steps - begin) * 3 // 8 // (nf - 1)
+    portion = 0
     rest = begin + portion * (nf - 1)
+    later = rest + (steps - rest) * 6 // 8
 
     def let_go():
         pl.semaphore_signal(go_sem, inc=1, device_id=(me_c, me_f + 1), device_id_type=MESH)
@@ -235,11 +258,9 @@
 
         @pl.loop(0, nf)
         def _(k):
-            send_far(partner(k))
-
-        @pl.loop(0, nf)
-        def _(k):
-            send_near(partner(k))
+            j = partner(k)
+            for offset in (1, -1):
+                pl.when(there(offset))(own_copy(j, offset).start)
 
     def run_first():
         make_operator(0, begin)
@@ -249,7 +270,8 @@
             j = partner(k)
             plane_arrival(j).wait_recv()
             send_far(j)
-            make_operator(begin + (k - 1) * portion, begin + k * portion)
+            if portion:
+                make_operator(begin + (k - 1) * portion, begin + k * portion)
 
         send_near(me_f, True)
 
@@ -263,7 +285,7 @@
         pl.when(second)(run_second)
     if_first(run_first)
 
-    @pl.loop(REACH, nc - 1)
+    @pl.loop(reach, nc - 1)
     def _(hop):
         block = jnp.where(me_c >= hop, me_c - hop, me_c + hop)
         other = jnp.where(me_c >= hop, me_c + hop, nc)
@@ -278,23 +300,18 @@
                     relay_copy(which, j).start()
 
             def early():
-                @pl.when(k < halves)
-                def _():
-                    make_operator(rest + lax.div((steps - rest) * k, halves), rest + lax.div((steps - rest) * (k + 1), halves))
-
-                @pl.when(k >= halves)
-                def _():
-                    multiply_step(me_c, k - halves, first=True)
+                make_operator(rest + lax.div((later - rest) * k, nf), rest + lax.div((later - rest) * (k + 1), nf))
 
             if_first(early, hop == REACH)
             if stagger:
                 if_first(let_go, hop == REACH, k == GO_AT * nf // 8)
 
     if nc <= REACH + 1:
-        if_first(lambda: make_operator(rest, steps))
-        if_first(lambda: multiply(me_c, first=True))
+        if_first(lambda: make_operator(rest, later))
         if stagger:
             if_first(let_go)
+    if_first(lambda: make_operator(later, steps))
+    if_first(lambda: multiply(me_c, first=True))
 
     lower = 2 * me_c < nc
     depth = jnp.where(lower, me_c, nc - 1 - me_c)
@@ -304,10 +321,10 @@
         place = jnp.where(depth == 0, turn, place)
         return jnp.where(lower, place, nc - 1 - place)
 
-    def arrive(block):
+    def arrive(block, low=0, high=nf):
         @pl.when(jnp.logical_not(passed_on(block)))
         def _():
-            @pl.loop(0, nf)
+            @pl.loop(low, high)
             def _(k):
                 j = partner(k)
                 line_copy(block, j, block, relay_send.at[block * nf + j]).wait_recv()
@@ -318,8 +335,12 @@
         arrive(block)
         multiply(block)
 
-    arrive(block_in_turn(nc - 1))
-    multiply(block_in_turn(nc - 1), last=True)
+    block = block_in_turn(nc - 1)
+    near = lax.div(me_f, nf // 2)
+    arrive(block, 0, nf // 2)
+    multiply(block, last=True, part_of=near)
+    arrive(block, nf // 2, nf)
+    multiply(block, last=True, part_of=1 - near)
 
     real, imag = vols[:frames, :], vols[frames:, :]
     both = jnp.concatenate([real, imag], axis=1)
@@ -384,10 +405,10 @@
     same = down == across
     g_re = jnp.where(down <= across, packed, turned)
     g_im = jnp.where(down > across, packed, jnp.where(same, 0.0, -turned))
-    squares = packed * packed
-    squares = jnp.where(same, squares, squares + squares)
-    squares = jnp.sum(jnp.sum(squares, axis=0, keepdims=True), axis=1, keepdims=True)
-    factor = 4.0 / jnp.sqrt(squares + EPSILON)
+    norm = packed * packed
+    norm = jnp.where(same, norm, norm + norm)
+    norm = jnp.sum(jnp.sum(norm, axis=0, keepdims=True), axis=1, keepdims=True)
+    factor = 4.0 / jnp.sqrt(norm + EPSILON)
     first = jnp.concatenate([g_re, g_im], axis=1).astype(BF16)
     below = jnp.concatenate([-g_im, g_re], axis=1).astype(BF16)
     rhs = jnp.concatenate([first, below], axis=0)
@@ -430,7 +451,9 @@
     def _(j):
         for offset in range(1, REACH + 1):
             for signed in (offset, -offset):
-                @pl.when(there(signed))
+                sent_it = there(signed) if offset == 1 else jnp.logical_and(there(signed), reach >= offset)
+
+                @pl.when(sent_it)
                 def _():
                     own_copy(j, signed).wait_send()
 
@@ -486,8 +509,10 @@
             pltpu.VMEM(vox_pos.shape, vox_pos.dtype),
             pltpu.SMEM(subbands.shape, subbands.dtype),
             dma((3,)),
-            pltpu.VMEM((3, chans, LANES), F32),
-            pltpu.VMEM((3, vd), F32),
+            pltpu.VMEM((chans, LANES), BF16),
+            pltpu.VMEM((chans, LANES), F32),
+            pltpu.VMEM((1, vd), F32),
+            pltpu.VMEM((chans, vd), F32),
             pltpu.VMEM((2, chans, vd), BF16),
             pltpu.VMEM((2 * frames, vd), F32),
             pltpu.VMEM((2 * frames, vd), BF16),

time: 48.3 us -> 47.4 us (0.981)
  Pallas kernels: 46.2 us -> 45.3 us
    pallas_call x1, Pallas kernels: 46.2 us -> 45.3 us  [shards(): pl.pallas_call(functools.partial(kernel, nc, nf, nbins), out_shape=pltpu....]
where the time goes in v2:
time: 47.4 us; the launch traced here: 46.9 us
  Pallas kernels  45.3 us (96%)
  local copies, waits for them, and re-layouts  1.55 us (3%)
    pallas_call x1, Pallas kernels, shards(): pl.pallas_call(functools.partial(kernel, nc, nf, nbins), out_shape=pltpu....  45.3 us
    reshape x1, local copies, waits for them, and re-layouts, shards(): return jnp.transpose(received, (3, 2, 0, 1, 4)).reshape(fl, 2, nbins, vl)  1.55 us

profile of v2, /device:TPU:1, one launch (start us, length us, event | category | flops | bytes accessed | tf_op | source)
XLA Modules:
  0.0 46.9 jit_solution(12816821667973752815)
XLA Ops:
  0.0 45.3 %shard_map.46 = bf16[8,2,32,1024]{3,2,1,0:T(8,128)(2,1)S(1)} custom-call(bf16[2,8,32,256]{3,2,1,0:T(8,128)(2,1)} %rf_ref.1, s32[3,1024]{1,0:T(4,128)} %elem_hbm.1, s32[3,1024]{1,0:T(4,128)} %vox_hbm.1, s32[8]{0:T(128)} %sub_hbm.1), custom_call_target="tpu_custom_call" | custom-call | tf_op jit(solution)/shard_map/pallas_call | solution.py:501
  45.3 1.5 %copy.5 = bf16[32,2,8,1024]{3,2,1,0:T(8,128)(2,1)} copy(bf16[32,2,8,1024]{3,0,1,2:T(8,128)(2,1)S(1)} %bitcast.5) | data formatting | bytes 2097152 | tf_op jit(solution)/shard_map/reshape | solution.py:533

commit v3 on v2

--- a/solution.py
+++ b/solution.py
@@ -41,7 +41,7 @@
     nc, nf, nbins,
     rf_ref, elem_hbm, vox_hbm, sub_hbm, out_ref,
     rfbuf, elem_ref, vox_ref, sub_ref, in_sem, elem, heights, vox, squares, oper, acc, vols, part, slabs, total, hmat, sent,
-    go_sem, own_sem, plane_send, plane_recv, line_send, relay_send, line_recv,
+    met_sem, go_sem, own_sem, plane_send, plane_recv, line_send, relay_send, line_recv,
     rs_send, rs_recv, ag_send, ag_recv, out_own, out_send, out_recv,
 ):
     share = nf // nbins
@@ -79,13 +79,17 @@
     def piece(j):
         return pl.ds(pl.multiple_of(j * fl, fl), fl)
 
+    base_f = me_f - lax.rem(me_f, 2)
     barrier = pltpu.get_barrier_semaphore()
-    for k in range(1, nf):
-        pl.semaphore_signal(barrier, inc=1, device_id=(me_c, partner(k)), device_id_type=MESH)
-    for k in range(1, nc):
-        for s in range(share):
-            other = (lax.rem(me_c + k, nc), me_bin * share + s)
-            pl.semaphore_signal(barrier, inc=1, device_id=other, device_id_type=MESH)
+    for step in range(2, nf, 2):
+        pl.semaphore_signal(barrier, inc=1, device_id=(me_c, lax.rem(base_f + step, nf)), device_id_type=MESH)
+
+    @pl.when(second)
+    def _():
+        pl.semaphore_signal(barrier, inc=1, device_id=(me_c, base_f), device_id_type=MESH)
+
+    for step in range(1, nc):
+        pl.semaphore_signal(barrier, inc=1, device_id=(lax.rem(me_c + step, nc), base_f + 1), device_id_type=MESH)
 
     mine = piece(me_f)
     loads = [
@@ -97,7 +101,15 @@
         load.start()
     own = pltpu.make_async_copy(rf_ref.at[:, me_bin], rfbuf.at[me_c, :, mine], own_sem)
     own.start()
-    pl.semaphore_wait(barrier, nf - 1 + (nc - 1) * share)
+
+    @pl.when(first_core)
+    def _():
+        pl.semaphore_wait(barrier, nf - 1)
+        pl.semaphore_signal(met_sem, inc=1, device_id=(me_c, base_f + 1), device_id_type=MESH)
+
+    @pl.when(second)
+    def _():
+        pl.semaphore_wait(met_sem, 1)
 
     def plane_copy(j):
         return pltpu.make_async_remote_copy(
@@ -147,8 +159,6 @@
                 def _():
                     own_copy(j, signed, mine_too).start()
 
-    if_first(lambda: send_far(me_f, True))
-    base_f = me_f - lax.rem(me_f, 2)
     for parity in (0, 1):
         for k in range(0, nf, 2):
             j = lax.rem(base_f + k, nf) + parity
@@ -158,6 +168,17 @@
                     plane_copy(j).start()
             else:
                 plane_copy(j).start()
+
+    @pl.when(first_core)
+    def _():
+        pl.semaphore_wait(met_sem, 1)
+
+    @pl.when(second)
+    def _():
+        pl.semaphore_wait(barrier, (nc - 1) * 2)
+        pl.semaphore_signal(met_sem, inc=1, device_id=(me_c, base_f), device_id_type=MESH)
+
+    if_first(lambda: send_far(me_f, True))
 
     scale = 2.0 / math.sqrt(chans)
     sin_poly = [coef * math.sqrt(scale) * BELOW_ONE for coef in SIN_POLY]
@@ -233,14 +254,27 @@
             else:
                 acc[where, :] = some
 
+    width = vd // (nf // 2)
+
+    def multiply_step(block, step):
+        place = pl.ds(pl.multiple_of(block * cl, cl), cl)
+        lanes = pl.ds(pl.multiple_of(step * width, width), width)
+        real, imag = rfbuf[block, 0], rfbuf[block, 1]
+        left = jnp.concatenate(
+            [jnp.concatenate([real, imag], axis=1), jnp.concatenate([imag, -real], axis=1)], axis=0)
+        acc[:, lanes] = acc[:, lanes] + dot(left, jnp.concatenate([oper[0, place, lanes], oper[1, place, lanes]], axis=0))
+
+    pairs = stagger and nc == 4
+    inside = jnp.logical_and(second, jnp.logical_and(me_c > 0, me_c < nc - 1))
+
     def passed_on(block):
         right = jnp.logical_and(me_c - block >= reach, me_c < nc - 1)
         return jnp.logical_or(right, jnp.logical_and(block - me_c >= reach, me_c > 0))
 
     begin = steps // 8
-    portion = 0
+    portion = steps * 1 // 32
     rest = begin + portion * (nf - 1)
-    later = rest + (steps - rest) * 6 // 8
+    later = rest + (steps - rest) * 8 // 8
 
     def let_go():
         pl.semaphore_signal(go_sem, inc=1, device_id=(me_c, me_f + 1), device_id_type=MESH)
@@ -303,6 +337,11 @@
                 make_operator(rest + lax.div((later - rest) * k, nf), rest + lax.div((later - rest) * (k + 1), nf))
 
             if_first(early, hop == REACH)
+            if pairs:
+                @pl.when(jnp.logical_and(inside, hop == 2))
+                def _():
+                    upper = lax.div(2 * k, nf)
+                    multiply_step(me_c - 1 + 2 * upper, k - upper * (nf // 2))
             if stagger:
                 if_first(let_go, hop == REACH, k == GO_AT * nf // 8)
 
@@ -329,13 +368,13 @@
                 j = partner(k)
                 line_copy(block, j, block, relay_send.at[block * nf + j]).wait_recv()
 
-    @pl.loop(1, nc - 1)
+    @pl.loop(1, jnp.where(inside, 1, nc - 1) if pairs else nc - 1)
     def _(turn):
         block = block_in_turn(turn)
         arrive(block)
         multiply(block)
 
-    block = block_in_turn(nc - 1)
+    block = block_in_turn(jnp.where(inside, 2, nc - 1) if pairs else nc - 1)
     near = lax.div(me_f, nf // 2)
     arrive(block, 0, nf // 2)
     multiply(block, last=True, part_of=near)
@@ -401,7 +440,7 @@
             gather(index, owners[index]).wait_recv()
 
     packed = total[...].astype(F32)
-    turned = packed.T
+    turned = total[...].T.astype(F32)
     same = down == across
     g_re = jnp.where(down <= across, packed, turned)
     g_im = jnp.where(down > across, packed, jnp.where(same, 0.0, -turned))
@@ -413,9 +452,7 @@
     below = jnp.concatenate([-g_im, g_re], axis=1).astype(BF16)
     rhs = jnp.concatenate([first, below], axis=0)
     second_power = dot(first, rhs)
-    high = second_power.astype(BF16)
-    low = (second_power - high.astype(F32)).astype(BF16)
-    third_power = dot(high, rhs) + dot(low, rhs)
+    third_power = dot(second_power.astype(BF16), rhs)
     poly = factor * (factor * (0.3 * second_power - (0.03 * factor) * third_power) - first.astype(F32))
     h_re = (jnp.where(same, 1.0, 0.0) + poly[:, :frames]).astype(BF16)
     h_im = poly[:, frames:].astype(BF16)
@@ -424,24 +461,26 @@
     hmat[frames:, :frames] = -h_im
     hmat[frames:, frames:] = h_re
 
-    def out_copy(j, chunk):
-        lanes = pl.ds(chunk * span, span)
+    def out_copy(j, arriving=False):
         return pltpu.make_async_remote_copy(
-            src_ref=sent.at[:, piece(j), lanes], dst_ref=out_ref.at[me_f, :, :, lanes],
-            send_sem=out_send.at[chunk * nf + j], recv_sem=out_recv.at[chunk * nf + me_f],
+            src_ref=sent.at[:, piece(j)], dst_ref=out_ref.at[j if arriving else me_f],
+            send_sem=out_send.at[j], recv_sem=out_recv.at[j if arriving else me_f],
             device_id=(me_c, j), device_id_type=MESH)
 
-    chunks = out_own.shape[0]
-    span = vd // chunks
-    lhs = hmat[...]
-    for chunk in range(chunks):
-        lanes = pl.ds(chunk * span, span)
-        value = dot(lhs, vols[:, lanes]).astype(BF16)
-        sent[0, :, lanes] = value[:frames]
-        sent[1, :, lanes] = value[frames:]
-        for k in range(nf - 1, 0, -1):
-            out_copy(partner(k), chunk).start()
-        pltpu.make_async_copy(sent.at[:, mine, lanes], out_ref.at[me_f, :, :, lanes], out_own.at[chunk]).start()
+    height = 2 * fl
+    for k in range(nf - 2, -1, -2):
+        near, far = partner(k), partner(k + 1)
+        start = pl.multiple_of(lax.div(near, 2) * height, height)
+        place = pl.ds(start, height)
+        lhs = jnp.concatenate([hmat[place, :], hmat[pl.ds(frames + start, height), :]], axis=0)
+        value = dot(lhs, vols[...]).astype(BF16)
+        sent[0, place, :] = value[:height]
+        sent[1, place, :] = value[height:]
+        out_copy(far).start()
+        if k:
+            out_copy(near).start()
+    own_out = pltpu.make_async_copy(sent.at[:, mine], out_ref.at[me_f], out_own)
+    own_out.start()
 
     @pl.loop(1, nf)
     def _(k):
@@ -473,18 +512,13 @@
             for member in members:
                 if member != owners[index]:
                     gather(index, member).wait_send()
-    for chunk in range(chunks):
-        lanes = pl.ds(chunk * span, span)
-        pltpu.make_async_copy(sent.at[:, mine, lanes], out_ref.at[me_f, :, :, lanes], out_own.at[chunk]).wait()
-
-        @pl.loop(1, nf)
-        def _(k):
-            j = partner(k)
-            out_copy(j, chunk).wait_send()
-            pltpu.make_async_remote_copy(
-                src_ref=sent.at[:, mine, lanes], dst_ref=out_ref.at[j, :, :, lanes],
-                send_sem=out_send.at[chunk * nf + j], recv_sem=out_recv.at[chunk * nf + j],
-                device_id=(me_c, j), device_id_type=MESH).wait_recv()
+    own_out.wait()
+
+    @pl.loop(1, nf)
+    def _(k):
+        j = partner(k)
+        out_copy(j).wait_send()
+        out_copy(j, True).wait_recv()
 
 
 def shards(nc, nf, rf_data, elem_pos, vox_pos, subbands):
@@ -495,7 +529,6 @@
     vl = vox_pos.shape[1]
     vd = vl // share
     group = nc * share
-    chunks = 4
     dma = pltpu.SemaphoreType.DMA
     inputs = [pltpu.with_memory_space_constraint(x, pltpu.HBM) for x in (rf_data, elem_pos, vox_pos, subbands)]
     received = pl.pallas_call(
@@ -521,10 +554,10 @@
             pltpu.VMEM((frames, frames), BF16),
             pltpu.VMEM((2 * frames, 2 * frames), BF16),
             pltpu.VMEM((2, frames, vd), BF16),
-            pltpu.SemaphoreType.REGULAR, dma, dma((nf,)), dma((nf,)),
+            pltpu.SemaphoreType.REGULAR, pltpu.SemaphoreType.REGULAR, dma, dma((nf,)), dma((nf,)),
             dma((2 * REACH * nf,)), dma((nc * nf,)), dma((nc * nf,)),
             dma((2,)), dma((group,)), dma((group,)), dma((2,)),
-            dma((chunks,)), dma((chunks * nf,)), dma((chunks * nf,)),
+            dma, dma((nf,)), dma((nf,)),
         ],
         compiler_params=pltpu.CompilerParams(
             collective_id=0, has_side_effects=True, vmem_limit_bytes=40 * 2**20),

time: 47.4 us -> 46.6 us (0.983)
  no operation moved by 1% of the time
where the time goes in v3:
time: 46.6 us; the launch traced here: 46.4 us
  Pallas kernels  44.9 us (96%)
  local copies, waits for them, and re-layouts  1.55 us (3%)
    pallas_call x1, Pallas kernels, shards(): pl.pallas_call(functools.partial(kernel, nc, nf, nbins), out_shape=pltpu....  44.9 us
    reshape x1, local copies, waits for them, and re-layouts, shards(): return jnp.transpose(received, (3, 2, 0, 1, 4)).reshape(fl, 2, nbins, vl)  1.55 us

profile of v3, /device:TPU:1, one launch (start us, length us, event | category | flops | bytes accessed | tf_op | source)
XLA Modules:
  0.0 46.4 jit_solution(4484104639940544147)
XLA Ops:
  0.0 44.9 %shard_map.46 = bf16[8,2,32,1024]{3,2,1,0:T(8,128)(2,1)S(1)} custom-call(bf16[2,8,32,256]{3,2,1,0:T(8,128)(2,1)} %rf_ref.1, s32[3,1024]{1,0:T(4,128)} %elem_hbm.1, s32[3,1024]{1,0:T(4,128)} %vox_hbm.1, s32[8]{0:T(128)} %sub_hbm.1), custom_call_target="tpu_custom_call" | custom-call | tf_op jit(solution)/shard_map/pallas_call | solution.py:534
  44.9 1.5 %copy.5 = bf16[32,2,8,1024]{3,2,1,0:T(8,128)(2,1)} copy(bf16[32,2,8,1024]{3,0,1,2:T(8,128)(2,1)S(1)} %bitcast.5) | data formatting | bytes 2097152 | tf_op jit(solution)/shard_map/reshape | solution.py:566

commit v4 on v3

--- a/solution.py
+++ b/solution.py
@@ -16,7 +16,7 @@
 BELOW_ONE = 1.0 - 2e-6
 LANES = 128
 ROUND = 12582912.0
-TALL = 32
+TALL = 64
 REACH = 2
 GO_AT = 7
 SECOND_REACH = 1
@@ -180,6 +180,13 @@
 
     if_first(lambda: send_far(me_f, True))
 
+    def send_next(j, mine_too=False):
+        for offset in (1, -1):
+            pl.when(there(offset))(own_copy(j, offset, mine_too).start)
+
+    if stagger:
+        pl.when(second)(functools.partial(send_next, me_f, True))
+
     scale = 2.0 / math.sqrt(chans)
     sin_poly = [coef * math.sqrt(scale) * BELOW_ONE for coef in SIN_POLY]
     for load in loads:
@@ -272,7 +279,7 @@
         return jnp.logical_or(right, jnp.logical_and(block - me_c >= reach, me_c > 0))
 
     begin = steps // 8
-    portion = steps * 1 // 32
+    portion = 0
     rest = begin + portion * (nf - 1)
     later = rest + (steps - rest) * 8 // 8
 
@@ -280,9 +287,12 @@
         pl.semaphore_signal(go_sem, inc=1, device_id=(me_c, me_f + 1), device_id_type=MESH)
 
     def run_second():
-        make_operator(0, steps)
-
-        @pl.loop(1, nf)
+        make_operator(0, steps // 8)
+        plane_arrival(partner(1)).wait_recv()
+        send_next(partner(1))
+        make_operator(steps // 8, steps)
+
+        @pl.loop(2, nf)
         def _(k):
             plane_arrival(partner(k)).wait_recv()
 
@@ -290,11 +300,9 @@
         multiply(me_c, first=True)
         pl.semaphore_wait(go_sem, 1)
 
-        @pl.loop(0, nf)
+        @pl.loop(2, nf)
         def _(k):
-            j = partner(k)
-            for offset in (1, -1):
-                pl.when(there(offset))(own_copy(j, offset).start)
+            send_next(partner(k))
 
     def run_first():
         make_operator(0, begin)
@@ -319,7 +327,7 @@
         pl.when(second)(run_second)
     if_first(run_first)
 
-    @pl.loop(reach, nc - 1)
+    @pl.loop(jnp.where(inside, nc - 1, reach) if pairs else reach, nc - 1)
     def _(hop):
         block = jnp.where(me_c >= hop, me_c - hop, me_c + hop)
         other = jnp.where(me_c >= hop, me_c + hop, nc)
@@ -337,13 +345,27 @@
                 make_operator(rest + lax.div((later - rest) * k, nf), rest + lax.div((later - rest) * (k + 1), nf))
 
             if_first(early, hop == REACH)
-            if pairs:
-                @pl.when(jnp.logical_and(inside, hop == 2))
-                def _():
-                    upper = lax.div(2 * k, nf)
-                    multiply_step(me_c - 1 + 2 * upper, k - upper * (nf // 2))
             if stagger:
                 if_first(let_go, hop == REACH, k == GO_AT * nf // 8)
+
+    def pass_all_on():
+        low_side = 2 * me_c < nc
+        outer = jnp.where(low_side, me_c - 1, me_c + 1)
+        inner = jnp.where(low_side, me_c + 1, me_c - 1)
+        before = None
+        for block in (outer, inner, jnp.where(low_side, nc - 1, 0)):
+            @pl.loop(0, nf)
+            def _(k):
+                j = partner(k)
+                relay_copy(block, j).wait_recv()
+                relay_copy(block, j).start()
+                if before is not None:
+                    pl.when(k < nf // 2)(functools.partial(multiply_step, before, k))
+
+            before = block
+
+    if pairs:
+        pl.when(inside)(pass_all_on)
 
     if nc <= REACH + 1:
         if_first(lambda: make_operator(rest, later))

time: 46.6 us -> 45.9 us (0.985)
  Pallas kernels: 44.9 us -> 44.2 us
    pallas_call x1, Pallas kernels: 44.9 us -> 44.2 us  [shards(): pl.pallas_call(functools.partial(kernel, nc, nf, nbins), out_shape=pltpu....]
where the time goes in v4:
time: 45.9 us; the launch traced here: 45.8 us
  Pallas kernels  44.2 us (96%)
  local copies, waits for them, and re-layouts  1.55 us (3%)
    pallas_call x1, Pallas kernels, shards(): pl.pallas_call(functools.partial(kernel, nc, nf, nbins), out_shape=pltpu....  44.2 us
    reshape x1, local copies, waits for them, and re-layouts, shards(): return jnp.transpose(received, (3, 2, 0, 1, 4)).reshape(fl, 2, nbins, vl)  1.55 us

profile of v4, /device:TPU:1, one launch (start us, length us, event | category | flops | bytes accessed | tf_op | source)
XLA Modules:
  0.0 45.8 jit_solution(14470985746164738041)
XLA Ops:
  0.0 44.2 %shard_map.46 = bf16[8,2,32,1024]{3,2,1,0:T(8,128)(2,1)S(1)} custom-call(bf16[2,8,32,256]{3,2,1,0:T(8,128)(2,1)} %rf_ref.1, s32[3,1024]{1,0:T(4,128)} %elem_hbm.1, s32[3,1024]{1,0:T(4,128)} %vox_hbm.1, s32[8]{0:T(128)} %sub_hbm.1), custom_call_target="tpu_custom_call" | custom-call | tf_op jit(solution)/shard_map/pallas_call | solution.py:556
  44.2 1.5 %copy.5 = bf16[32,2,8,1024]{3,2,1,0:T(8,128)(2,1)} copy(bf16[32,2,8,1024]{3,0,1,2:T(8,128)(2,1)S(1)} %bitcast.5) | data formatting | bytes 2097152 | tf_op jit(solution)/shard_map/reshape | solution.py:588

commit v5 on v4

--- a/solution.py
+++ b/solution.py
@@ -287,10 +287,10 @@
         pl.semaphore_signal(go_sem, inc=1, device_id=(me_c, me_f + 1), device_id_type=MESH)
 
     def run_second():
-        make_operator(0, steps // 8)
+        make_operator(0, steps * 3 // 16)
         plane_arrival(partner(1)).wait_recv()
         send_next(partner(1))
-        make_operator(steps // 8, steps)
+        make_operator(steps * 3 // 16, steps)
 
         @pl.loop(2, nf)
         def _(k):

time: 45.9 us -> 45.9 us (level)
  no operation moved by 1% of the time
where the time goes in v5:
time: 45.9 us; the launch traced here: 45.8 us
  Pallas kernels  44.2 us (96%)
  local copies, waits for them, and re-layouts  1.55 us (3%)
    pallas_call x1, Pallas kernels, shards(): pl.pallas_call(functools.partial(kernel, nc, nf, nbins), out_shape=pltpu....  44.2 us
    reshape x1, local copies, waits for them, and re-layouts, shards(): return jnp.transpose(received, (3, 2, 0, 1, 4)).reshape(fl, 2, nbins, vl)  1.55 us

profile of v5, /device:TPU:1, one launch (start us, length us, event | category | flops | bytes accessed | tf_op | source)
XLA Modules:
  0.0 45.8 jit_solution(11270215246838112121)
XLA Ops:
  0.0 44.2 %shard_map.46 = bf16[8,2,32,1024]{3,2,1,0:T(8,128)(2,1)S(1)} custom-call(bf16[2,8,32,256]{3,2,1,0:T(8,128)(2,1)} %rf_ref.1, s32[3,1024]{1,0:T(4,128)} %elem_hbm.1, s32[3,1024]{1,0:T(4,128)} %vox_hbm.1, s32[8]{0:T(128)} %sub_hbm.1), custom_call_target="tpu_custom_call" | custom-call | tf_op jit(solution)/shard_map/pallas_call | solution.py:556
  44.2 1.5 %copy.5 = bf16[32,2,8,1024]{3,2,1,0:T(8,128)(2,1)} copy(bf16[32,2,8,1024]{3,0,1,2:T(8,128)(2,1)S(1)} %bitcast.5) | data formatting | bytes 2097152 | tf_op jit(solution)/shard_map/reshape | solution.py:588
